TPU v7x, 32 devices: a whole 2x2x4 slice. The times are simulated.
32 devices in a mesh: xs: 4 (over y, x), ax: 8 (over z, core).
Axes of the slice: x: 2, y: 2, z: 4, core: 2. Of those that a mesh axis runs over, the one named last changes fastest.
Arguments:
- concentration: float32 [256, 128, 384], P('ax', 'xs'), may hold values from -4 to 4
- tissue_mask: int32 [256, 128, 384], P('ax', 'xs'), may hold values from 0 to 1
- wall_layer: int32 [256, 128, 384], P('ax', 'xs'), may hold values from 0 to 3, as said below
- stiffness: float32 [256, 128, 384], P('ax', 'xs'), may hold values from 1 to 2
- production: float32 [256, 128, 384], P('ax', 'xs'), may hold values from -3 to 3
- layer_diffusivity: float32 [4], replicated, may hold values from 1 to 2
- uptake_rate: float32 [4], replicated, may hold values from 0.1 to 0.5
Outputs:
- concentration_out: float32 [256, 128, 384], P('ax', 'xs')
Inputs may be any that keep to these rules, and one draw needn't show every extreme that they name: `wall_layer`: indexes the tables of layer coefficients.
All inputs are finite; a program needn't handle non-finite values.
Results may differ from a plain program's by a relative error of at most 0.0003.
Values sent between devices are 32-bit elements; how exact they have to be, the bound alone decides.
A program may use at most 128 MiB of HBM per device.

v0:
```python
import functools

import jax
import jax.numpy as jnp
from jax import lax
from jax.experimental import pallas as pl
from jax.experimental.pallas import tpu as pltpu
from jax.sharding import PartitionSpec as P

STEPS = 2
RZ = 3072
SECTION_RATE = 0.05
MESH = pl.DeviceIdType.MESH


def lookup(labels, table_ref):
    summed = jnp.zeros(labels.shape, jnp.float32)
    for index in range(table_ref.shape[0]):
        summed = jnp.where(labels == index, table_ref[index], summed)
    return summed


def kernel(
    n_ax, n_xs, chunk,
    conc_hbm, mask_hbm, layer_hbm, stiff_hbm, prod_hbm, diff_tab, upt_tab,
    out_ref,
    mask, layer, stiff, source, state, root, ratio, recip, prodr, part, plane, side, uptake,
    edge, halo, fixed, shut, outer_in, inner_in, a_send, b_send, rows,
    in_sem, xs_send, xs_recv, ax_send, ax_recv, a_ssem, a_rsem, b_ssem, b_rsem,
):
    m, slab, cols = conc_hbm.shape
    chunks = slab // chunk
    me = lax.axis_index("ax")
    mx = lax.axis_index("xs")
    half = n_ax // 2
    lower = me < half
    inner = jnp.where(lower, me + 1, me - 1)
    outer = jnp.where(lower, me - 1, me + 1)
    middle = (me == half - 1) | (me == half)
    has_outer = (me > 0) & (me < n_ax - 1)

    loads = [
        pltpu.make_async_copy(src, dst, in_sem.at[at])
        for at, (src, dst) in enumerate(
            [(mask_hbm, mask), (layer_hbm, layer), (stiff_hbm, stiff), (conc_hbm, state), (prod_hbm, source)]
        )
    ]
    for load in loads:
        load.start()

    sides = (
        (mx > 0, {"xs": mx - 1}),
        (mx < n_xs - 1, {"xs": mx + 1}),
        (me > 0, {"ax": me - 1}),
        (me < n_ax - 1, {"ax": me + 1}),
    )
    barrier = pltpu.get_barrier_semaphore()
    for there, peer in sides:
        @pl.when(there)
        def _(peer=peer):
            pl.semaphore_signal(barrier, inc=1, device_id=peer, device_id_type=MESH)

    for at in range(2):
        @pl.when(jnp.logical_not(sides[at][0]))
        def _(at=at):
            for slot in range(STEPS + 1):
                halo[slot, at] = jnp.zeros((m, 1, cols), jnp.float32)

    @pl.when(jnp.logical_not(sides[2][0]))
    def _():
        root[0] = jnp.zeros((slab, cols), jnp.float32)

    @pl.when(jnp.logical_not(sides[3][0]))
    def _():
        root[m + 1] = jnp.zeros((slab, cols), jnp.float32)

    @pl.when(jnp.logical_not(has_outer))
    def _():
        for step in range(STEPS):
            for at in range(2):
                outer_in[step, at] = jnp.zeros((slab, cols), jnp.float32)

    def xs_copy(slot, at):
        return pltpu.make_async_remote_copy(
            src_ref=edge.at[slot, at], dst_ref=halo.at[slot, 1 - at],
            send_sem=xs_send.at[slot, at], recv_sem=xs_recv.at[slot, 1 - at],
            device_id=sides[at][1], device_id_type=MESH,
        )

    def xs_start(slot):
        for at in range(2):
            @pl.when(sides[at][0])
            def _(at=at):
                xs_copy(slot, at).start()

    def xs_wait(slot):
        for at in range(2):
            @pl.when(sides[at][0])
            def _(at=at):
                xs_copy(slot, 1 - at).wait_recv()
                xs_copy(slot, at).wait_send()

    def ax_copy(at):
        src, dst = ((1, m + 1), (m, 0))[at]
        return pltpu.make_async_remote_copy(
            src_ref=root.at[src], dst_ref=root.at[dst],
            send_sem=ax_send.at[at], recv_sem=ax_recv.at[1 - at],
            device_id=sides[2 + at][1], device_id_type=MESH,
        )

    def set_root(z):
        diffusivity = mask[z].astype(jnp.float32) * lookup(layer[z], diff_tab) * stiff[z]
        value = jnp.sqrt(diffusivity)
        root[z + 1] = value
        edge[STEPS, 0, z] = value[0:1]
        edge[STEPS, 1, z] = value[slab - 1:slab]

    for load in loads[:3]:
        load.wait()
    set_root(0)
    set_root(m - 1)
    pl.semaphore_wait(barrier, sum(jnp.where(there, 1, 0) for there, _ in sides))
    for at in range(2):
        @pl.when(sides[2 + at][0])
        def _(at=at):
            ax_copy(at).start()

    loads[3].wait()

    def copy_edges(z, carry):
        edge[0, 0, z] = state[z, 0:1]
        edge[0, 1, z] = state[z, slab - 1:slab]
        return carry

    lax.fori_loop(0, m, copy_edges, 0)
    xs_start(0)

    def root_body(z, carry):
        set_root(z)
        return carry

    lax.fori_loop(1, m - 1, root_body, 0)
    xs_start(STEPS)
    loads[4].wait()

    def cell_body(z, carry):
        weight = mask[z].astype(jnp.float32)
        uptake[z] = weight * lookup(layer[z], upt_tab)
        source[z] = weight * source[z]
        return carry

    lax.fori_loop(0, m, cell_body, 0)
    for at in range(2):
        @pl.when(sides[2 + at][0])
        def _(at=at):
            ax_copy(1 - at).wait_recv()
            ax_copy(at).wait_send()

    band_first = RZ * root[0] * root[1]
    rows[0] = band_first

    def factor_body(z, carry):
        excess, product, total = carry
        band = (RZ * root[z + 1]) * root[z + 2]
        inverse = 1.0 / (excess + band)
        ratio_now = band * inverse
        scaled = product * inverse
        ratio[z] = ratio_now
        recip[z] = inverse
        prodr[z] = scaled
        return 1.0 + ratio_now * excess, product * ratio_now, total + product * scaled

    ones = jnp.ones((slab, cols), jnp.float32)
    _, through_up, total = lax.fori_loop(0, m, factor_body, (1.0 + band_first, ones, 0.0 * ones))
    alpha_low = band_first * total
    alpha_high = through_up
    beta_low = band_first * prodr[m - 1]
    beta_high = ratio[m - 1]
    fixed[0] = jnp.where(lower, alpha_low, beta_high)
    fixed[1] = jnp.where(lower, alpha_high, beta_low)
    fixed[2] = jnp.where(lower, beta_low, alpha_high)
    fixed[3] = jnp.where(lower, beta_high, alpha_low)

    xs_wait(STEPS)
    row_at = lax.broadcasted_iota(jnp.int32, (slab, cols), 0)
    col_at = lax.broadcasted_iota(jnp.int32, (slab, cols), 1)

    def plane_body(z, carry):
        value = root[z + 1]
        scaled = SECTION_RATE * value
        above = jnp.where(row_at == 0, halo[STEPS, 0, z], pltpu.roll(value, 1, 0))
        plane[z] = scaled * above
        shut[z] = scaled[slab - 1:slab] * halo[STEPS, 1, z]
        side[z] = jnp.where(col_at == 0, 0.0, scaled * pltpu.roll(value, 1, 1))
        return carry

    lax.fori_loop(0, m, plane_body, 0)

    def a_copy(step, c, to_middle):
        cut = pl.ds(c * chunk, chunk)
        pick = pl.ds(0, 2 if step == 0 else 1)
        return pltpu.make_async_remote_copy(
            src_ref=a_send.at[step, pick, cut],
            dst_ref=(inner_in if to_middle else outer_in).at[step, pick, cut],
            send_sem=a_ssem.at[step, c],
            recv_sem=(b_rsem if to_middle else a_rsem).at[step, c],
            device_id={"ax": inner}, device_id_type=MESH,
        )

    def b_copy(step, c):
        cut = pl.ds(c * chunk, chunk)
        return pltpu.make_async_remote_copy(
            src_ref=b_send.at[step, 0, cut], dst_ref=inner_in.at[step, 0, cut],
            send_sem=b_ssem.at[step, c], recv_sem=b_rsem.at[step, c],
            device_id={"ax": outer}, device_id_type=MESH,
        )

    for step in range(STEPS):
        xs_wait(step)

        def forward_body(z, carry):
            moved, first = carry
            now = state[z]
            above = jnp.where(row_at == 0, halo[step, 0, z], pltpu.roll(now, 1, 0))
            flux = plane[z] * (above - now)
            closing = shut[z] * (now[slab - 1:slab] - halo[step, 1, z])
            below = jnp.where(row_at == slab - 1, closing, pltpu.roll(flux, slab - 1, 0))
            across = side[z] * (pltpu.roll(now, 1, 1) - now)
            explicit = now + ((flux - below) + (across - pltpu.roll(across, cols - 1, 1)))
            value = explicit + moved
            part[z] = recip[z] * value
            return ratio[z] * value, first + prodr[z] * value

        _, first = lax.fori_loop(0, m, forward_body, (0.0 * ones, 0.0 * ones))
        last = part[m - 1]
        rows[1] = jnp.where(lower, first, last)
        rows[2] = jnp.where(lower, last, first)

        for c in range(chunks):
            cut = slice(c * chunk, (c + 1) * chunk)

            @pl.when(has_outer)
            def _(step=step, c=c):
                a_copy(step, c, False).wait_recv()

            link = outer_in[0, 1, cut]
            if step == 0:
                gain = 1.0 / (1.0 - link * fixed[0, cut])
                fixed[4, cut] = gain
                a_send[0, 1, cut] = fixed[3, cut] + fixed[2, cut] * (gain * link * fixed[1, cut])
                fixed[5, cut] = gain * link * fixed[1, cut]
            known = fixed[4, cut] * (outer_in[step, 0, cut] + link * rows[1, cut])
            rows[3, cut] = known
            a_send[step, 0, cut] = rows[2, cut] + fixed[2, cut] * known

            @pl.when(middle)
            def _(step=step, c=c):
                a_copy(step, c, True).start()

            @pl.when(jnp.logical_not(middle))
            def _(step=step, c=c):
                a_copy(step, c, False).start()

        for c in range(chunks):
            cut = slice(c * chunk, (c + 1) * chunk)

            @pl.when(middle)
            def _(step=step, c=c, cut=cut):
                a_copy(step, c, True).wait_recv()
                own, own_link = a_send[step, 0, cut], a_send[0, 1, cut]
                far, far_link = inner_in[step, 0, cut], inner_in[0, 1, cut]
                if step == 0:
                    fixed[6, cut] = 1.0 / (1.0 - own_link * far_link)
                rows[4, cut] = far + far_link * ((own + own_link * far) * fixed[6, cut])

            @pl.when(jnp.logical_not(middle))
            def _(step=step, c=c, cut=cut):
                b_copy(step, c).wait_recv()
                rows[4, cut] = inner_in[step, 0, cut]

            inner_value = rows[4, cut]
            outer_value = rows[3, cut] + fixed[5, cut] * inner_value
            rows[5, cut] = outer_value
            b_send[step, 0, cut] = rows[1, cut] + fixed[0, cut] * outer_value + fixed[1, cut] * inner_value

            @pl.when(has_outer)
            def _(step=step, c=c):
                b_copy(step, c).start()

        below_value = rows[0] * jnp.where(lower, rows[5], rows[4])
        above_value = jnp.where(lower, rows[4], rows[5])
        final = step == STEPS - 1

        def backward_body(at, later):
            z = m - 1 - at
            solved = part[z] + prodr[z] * below_value + ratio[z] * later
            after = solved + (source[z] - uptake[z] * solved)
            if final:
                out_ref[z] = after
            else:
                state[z] = after
                edge[step + 1, 0, z] = after[0:1]
                edge[step + 1, 1, z] = after[slab - 1:slab]
            return solved

        lax.fori_loop(0, m, backward_body, above_value)
        if not final:
            xs_start(step + 1)

    for step in range(STEPS):
        for c in range(chunks):
            a_copy(step, c, False).wait_send()

            @pl.when(has_outer)
            def _(step=step, c=c):
                b_copy(step, c).wait_send()


def on_device(n_ax, n_xs, conc, mask, layer, stiff, prod, diff_tab, upt_tab):
    m, slab, cols = conc.shape
    chunk = 8 if slab % 8 == 0 else slab
    chunks = slab // chunk
    f32 = jnp.float32
    cells = pltpu.VMEM((m, slab, cols), f32)
    labels = pltpu.VMEM((m, slab, cols), jnp.int32)
    dma = pltpu.SemaphoreType.DMA
    vmem = lambda *shape: pltpu.VMEM(shape, f32)
    any_spec = pl.BlockSpec(memory_space=pl.ANY)
    smem_spec = pl.BlockSpec(memory_space=pltpu.SMEM)
    return pl.pallas_call(
        functools.partial(kernel, n_ax, n_xs, chunk),
        out_shape=jax.ShapeDtypeStruct((m, slab, cols), f32),
        in_specs=[any_spec] * 5 + [smem_spec] * 2,
        out_specs=pl.BlockSpec(memory_space=pltpu.VMEM),
        scratch_shapes=[
            labels, labels, cells, cells, cells, vmem(m + 2, slab, cols),
            cells, cells, cells, cells, cells, cells, cells,
            vmem(STEPS + 1, 2, m, 1, cols), vmem(STEPS + 1, 2, m, 1, cols),
            vmem(7, slab, cols), vmem(m, 1, cols),
            vmem(STEPS, 2, slab, cols), vmem(STEPS, 2, slab, cols),
            vmem(STEPS, 2, slab, cols), vmem(STEPS, 1, slab, cols), vmem(6, slab, cols),
            dma((5,)), dma((STEPS + 1, 2)), dma((STEPS + 1, 2)), dma((2,)), dma((2,)),
            dma((STEPS, chunks)), dma((STEPS, chunks)), dma((STEPS, chunks)), dma((STEPS, chunks)),
        ],
        compiler_params=pltpu.CompilerParams(
            collective_id=0, has_side_effects=True, vmem_limit_bytes=56 * 1024 * 1024
        ),
    )(conc, mask, layer, stiff, prod, diff_tab, upt_tab)


def solution(mesh):
    cells = P("ax", "xs", None)
    return jax.shard_map(
        functools.partial(on_device, mesh.shape["ax"], mesh.shape["xs"]),
        mesh=mesh, in_specs=(cells,) * 5 + (P(), P()), out_specs=cells, check_vma=False,
    )
```

profile of v0, /device:TPU:0, one launch (start us, length us, event | category | flops | bytes accessed | tf_op | source)
XLA Modules:
  0.0 56.4 jit_solution(603697952198413534)
XLA Ops:
  0.0 53.7 %shard_map.73 = f32[32,32,384]{2,1,0:T(8,128)} custom-call(f32[32,32,384]{2,1,0:T(8,128)} %conc_hbm.1, s32[32,32,384]{2,1,0:T(8,128)} %mask_hbm.1, s32[32,32,384]{2,1,0:T(8,128)} %layer_hbm.1, f32[32,32,384]{2,1,0:T(8,128)} %stiff_hbm.1, f32[32,32,384]{2,1,0:T(8,128)} %prod_hbm.1, f32[4]{0:T(128)} %diff_tab.1, f32[4]{0:T(128)} %upt_tab.1), custom_call_target="tpu_custom_call" | custom-call | tf_op jit(solution)/shard_map/pallas_call | solution.py:330
  53.7 2.7 %copy.9 = f32[32,32,384]{2,1,0:T(8,128)} copy(f32[32,32,384]{2,1,0:T(8,128)} %shard_map.73) | data formatting | bytes 3145728
where the time goes:
time: 56.5 us; the launch traced here: 56.4 us
  Pallas kernels  53.7 us (95%)
  local copies, waits for them, and re-layouts  2.65 us (5%)
    pallas_call x1, Pallas kernels, on_device(): pl.pallas_call(functools.partial(kernel, n_ax, n_xs, chunk), out_shape=ja...  53.7 us
    unnamed x1, local copies, waits for them, and re-layouts  2.65 us

commit v1 on v0

--- a/solution.py
+++ b/solution.py
@@ -139,17 +139,8 @@
         set_root(z)
         return carry
 
-    lax.fori_loop(1, m - 1, root_body, 0)
+    lax.fori_loop(1, m - 1, root_body, 0, unroll=2)
     xs_start(STEPS)
-    loads[4].wait()
-
-    def cell_body(z, carry):
-        weight = mask[z].astype(jnp.float32)
-        uptake[z] = weight * lookup(layer[z], upt_tab)
-        source[z] = weight * source[z]
-        return carry
-
-    lax.fori_loop(0, m, cell_body, 0)
     for at in range(2):
         @pl.when(sides[2 + at][0])
         def _(at=at):
@@ -171,7 +162,7 @@
         return 1.0 + ratio_now * excess, product * ratio_now, total + product * scaled
 
     ones = jnp.ones((slab, cols), jnp.float32)
-    _, through_up, total = lax.fori_loop(0, m, factor_body, (1.0 + band_first, ones, 0.0 * ones))
+    _, through_up, total = lax.fori_loop(0, m, factor_body, (1.0 + band_first, ones, 0.0 * ones), unroll=2)
     alpha_low = band_first * total
     alpha_high = through_up
     beta_low = band_first * prodr[m - 1]
@@ -194,7 +185,7 @@
         side[z] = jnp.where(col_at == 0, 0.0, scaled * pltpu.roll(value, 1, 1))
         return carry
 
-    lax.fori_loop(0, m, plane_body, 0)
+    lax.fori_loop(0, m, plane_body, 0, unroll=2)
 
     def a_copy(step, c, to_middle):
         cut = pl.ds(c * chunk, chunk)
@@ -215,28 +206,59 @@
             device_id={"ax": outer}, device_id_type=MESH,
         )
 
+    loads[4].wait()
+
+    def cell_body(z, carry):
+        weight = mask[z].astype(jnp.float32)
+        uptake[z] = weight * lookup(layer[z], upt_tab)
+        source[z] = weight * source[z]
+        return carry
+
+    def cell_loop():
+        lax.fori_loop(0, m, cell_body, 0, unroll=2)
+
+    if chunks > 2:
+        inside = ((chunk, slab - chunk),)
+        ends = ((0, chunk), (slab - chunk, slab))
+        order = tuple(range(1, chunks - 1)) + (0, chunks - 1)
+    else:
+        inside, ends, order = (), ((0, slab),), tuple(range(chunks))
+    early = order[:chunks - 2] if inside else ()
+
     for step in range(STEPS):
-        xs_wait(step)
-
-        def forward_body(z, carry):
-            moved, first = carry
-            now = state[z]
-            above = jnp.where(row_at == 0, halo[step, 0, z], pltpu.roll(now, 1, 0))
-            flux = plane[z] * (above - now)
-            closing = shut[z] * (now[slab - 1:slab] - halo[step, 1, z])
-            below = jnp.where(row_at == slab - 1, closing, pltpu.roll(flux, slab - 1, 0))
-            across = side[z] * (pltpu.roll(now, 1, 1) - now)
-            explicit = now + ((flux - below) + (across - pltpu.roll(across, cols - 1, 1)))
-            value = explicit + moved
-            part[z] = recip[z] * value
-            return ratio[z] * value, first + prodr[z] * value
-
-        _, first = lax.fori_loop(0, m, forward_body, (0.0 * ones, 0.0 * ones))
-        last = part[m - 1]
-        rows[1] = jnp.where(lower, first, last)
-        rows[2] = jnp.where(lower, last, first)
-
-        for c in range(chunks):
+
+        def forward(ranges):
+            def body(z, carries):
+                done = []
+                for (lo, hi), (moved, first) in zip(ranges, carries):
+                    span = slice(lo, hi)
+                    size = hi - lo
+                    row = lax.broadcasted_iota(jnp.int32, (size, cols), 0)
+                    now = state[z, span]
+                    before = halo[step, 0, z] if lo == 0 else state[z, lo - 1:lo]
+                    above = jnp.where(row == 0, before, pltpu.roll(now, 1, 0))
+                    flux = plane[z, span] * (above - now)
+                    if hi == slab:
+                        closing = shut[z] * (now[size - 1:size] - halo[step, 1, z])
+                    else:
+                        closing = plane[z, hi:hi + 1] * (now[size - 1:size] - state[z, hi:hi + 1])
+                    below = jnp.where(row == size - 1, closing, pltpu.roll(flux, size - 1, 0))
+                    across = side[z, span] * (pltpu.roll(now, 1, 1) - now)
+                    explicit = now + ((flux - below) + (across - pltpu.roll(across, cols - 1, 1)))
+                    value = explicit + moved
+                    part[z, span] = recip[z, span] * value
+                    done.append((ratio[z, span] * value, first + prodr[z, span] * value))
+                return tuple(done)
+
+            zeros = [jnp.zeros((hi - lo, cols), jnp.float32) for lo, hi in ranges]
+            sums = lax.fori_loop(0, m, body, tuple((zero, zero) for zero in zeros), unroll=2)
+            for (lo, hi), (_, first) in zip(ranges, sums):
+                span = slice(lo, hi)
+                last = part[m - 1, span]
+                rows[1, span] = jnp.where(lower, first, last)
+                rows[2, span] = jnp.where(lower, last, first)
+
+        def inward(c):
             cut = slice(c * chunk, (c + 1) * chunk)
 
             @pl.when(has_outer)
@@ -261,7 +283,32 @@
             def _(step=step, c=c):
                 a_copy(step, c, False).start()
 
-        for c in range(chunks):
+        if inside:
+            forward(inside)
+
+            @pl.when(jnp.logical_not(has_outer))
+            def _():
+                for c in early:
+                    inward(c)
+
+        xs_wait(step)
+        forward(ends)
+        if step == 0:
+            pl.when(has_outer)(cell_loop)
+
+        @pl.when(has_outer)
+        def _():
+            for c in order:
+                inward(c)
+
+        @pl.when(jnp.logical_not(has_outer))
+        def _():
+            for c in order[len(early):]:
+                inward(c)
+            if step == 0:
+                cell_loop()
+
+        for c in order:
             cut = slice(c * chunk, (c + 1) * chunk)
 
             @pl.when(middle)
@@ -287,25 +334,43 @@
             def _(step=step, c=c):
                 b_copy(step, c).start()
 
-        below_value = rows[0] * jnp.where(lower, rows[5], rows[4])
-        above_value = jnp.where(lower, rows[4], rows[5])
         final = step == STEPS - 1
 
-        def backward_body(at, later):
-            z = m - 1 - at
-            solved = part[z] + prodr[z] * below_value + ratio[z] * later
-            after = solved + (source[z] - uptake[z] * solved)
-            if final:
-                out_ref[z] = after
-            else:
-                state[z] = after
-                edge[step + 1, 0, z] = after[0:1]
-                edge[step + 1, 1, z] = after[slab - 1:slab]
-            return solved
-
-        lax.fori_loop(0, m, backward_body, above_value)
-        if not final:
+        def backward(ranges):
+            lows = []
+            highs = []
+            for lo, hi in ranges:
+                span = slice(lo, hi)
+                lows.append(rows[0, span] * jnp.where(lower, rows[5, span], rows[4, span]))
+                highs.append(jnp.where(lower, rows[4, span], rows[5, span]))
+
+            def body(at, carries):
+                z = m - 1 - at
+                done = []
+                for (lo, hi), low, later in zip(ranges, lows, carries):
+                    span = slice(lo, hi)
+                    solved = part[z, span] + prodr[z, span] * low + ratio[z, span] * later
+                    after = solved + (source[z, span] - uptake[z, span] * solved)
+                    if final:
+                        out_ref[z, span] = after
+                    else:
+                        state[z, span] = after
+                        if lo == 0:
+                            edge[step + 1, 0, z] = after[0:1]
+                        if hi == slab:
+                            edge[step + 1, 1, z] = after[hi - lo - 1:hi - lo]
+                    done.append(solved)
+                return tuple(done)
+
+            lax.fori_loop(0, m, body, tuple(highs), unroll=2)
+
+        if final:
+            backward(((0, slab),))
+        else:
+            backward(ends)
             xs_start(step + 1)
+            if inside:
+                backward(inside)
 
     for step in range(STEPS):
         for c in range(chunks):

time: 56.5 us -> 51.2 us (0.906)
  Pallas kernels: 53.7 us -> 48.4 us
    pallas_call x1, Pallas kernels: 53.7 us -> 48.4 us  [on_device(): pl.pallas_call(functools.partial(kernel, n_ax, n_xs, chunk), out_shape=ja...]
where the time goes in v1:
time: 51.2 us; the launch traced here: 51 us
  Pallas kernels  48.4 us (95%)
  local copies, waits for them, and re-layouts  2.65 us (5%)
    pallas_call x1, Pallas kernels, on_device(): pl.pallas_call(functools.partial(kernel, n_ax, n_xs, chunk), out_shape=ja...  48.4 us
    unnamed x1, local copies, waits for them, and re-layouts  2.65 us

profile of v1, /device:TPU:0, one launch (start us, length us, event | category | flops | bytes accessed | tf_op | source)
XLA Modules:
  0.0 51.0 jit_solution(7273213730484548468)
XLA Ops:
  0.0 48.4 %shard_map.73 = f32[32,32,384]{2,1,0:T(8,128)} custom-call(f32[32,32,384]{2,1,0:T(8,128)} %conc_hbm.1, s32[32,32,384]{2,1,0:T(8,128)} %mask_hbm.1, s32[32,32,384]{2,1,0:T(8,128)} %layer_hbm.1, f32[32,32,384]{2,1,0:T(8,128)} %stiff_hbm.1, f32[32,32,384]{2,1,0:T(8,128)} %prod_hbm.1, f32[4]{0:T(128)} %diff_tab.1, f32[4]{0:T(128)} %upt_tab.1), custom_call_target="tpu_custom_call" | custom-call | tf_op jit(solution)/shard_map/pallas_call | solution.py:395
  48.4 2.7 %copy.9 = f32[32,32,384]{2,1,0:T(8,128)} copy(f32[32,32,384]{2,1,0:T(8,128)} %shard_map.73) | data formatting | bytes 3145728

commit v2 on v1

--- a/solution.py
+++ b/solution.py
@@ -132,14 +132,14 @@
         edge[0, 1, z] = state[z, slab - 1:slab]
         return carry
 
-    lax.fori_loop(0, m, copy_edges, 0)
+    lax.fori_loop(0, m, copy_edges, 0, unroll=8)
     xs_start(0)
 
     def root_body(z, carry):
         set_root(z)
         return carry
 
-    lax.fori_loop(1, m - 1, root_body, 0, unroll=2)
+    lax.fori_loop(1, m - 1, root_body, 0, unroll=6)
     xs_start(STEPS)
     for at in range(2):
         @pl.when(sides[2 + at][0])
@@ -162,7 +162,7 @@
         return 1.0 + ratio_now * excess, product * ratio_now, total + product * scaled
 
     ones = jnp.ones((slab, cols), jnp.float32)
-    _, through_up, total = lax.fori_loop(0, m, factor_body, (1.0 + band_first, ones, 0.0 * ones), unroll=2)
+    _, through_up, total = lax.fori_loop(0, m, factor_body, (1.0 + band_first, ones, 0.0 * ones), unroll=8)
     alpha_low = band_first * total
     alpha_high = through_up
     beta_low = band_first * prodr[m - 1]
@@ -185,7 +185,7 @@
         side[z] = jnp.where(col_at == 0, 0.0, scaled * pltpu.roll(value, 1, 1))
         return carry
 
-    lax.fori_loop(0, m, plane_body, 0, unroll=2)
+    lax.fori_loop(0, m, plane_body, 0, unroll=8)
 
     def a_copy(step, c, to_middle):
         cut = pl.ds(c * chunk, chunk)
@@ -215,7 +215,7 @@
         return carry
 
     def cell_loop():
-        lax.fori_loop(0, m, cell_body, 0, unroll=2)
+        lax.fori_loop(0, m, cell_body, 0, unroll=8)
 
     if chunks > 2:
         inside = ((chunk, slab - chunk),)
@@ -251,7 +251,7 @@
                 return tuple(done)
 
             zeros = [jnp.zeros((hi - lo, cols), jnp.float32) for lo, hi in ranges]
-            sums = lax.fori_loop(0, m, body, tuple((zero, zero) for zero in zeros), unroll=2)
+            sums = lax.fori_loop(0, m, body, tuple((zero, zero) for zero in zeros), unroll=8)
             for (lo, hi), (_, first) in zip(ranges, sums):
                 span = slice(lo, hi)
                 last = part[m - 1, span]
@@ -362,7 +362,7 @@
                     done.append(solved)
                 return tuple(done)
 
-            lax.fori_loop(0, m, body, tuple(highs), unroll=2)
+            lax.fori_loop(0, m, body, tuple(highs), unroll=8)
 
         if final:
             backward(((0, slab),))

time: 51.2 us -> 45.3 us (0.88)
  Pallas kernels: 48.4 us -> 42.5 us
    pallas_call x1, Pallas kernels: 48.4 us -> 42.5 us  [on_device(): pl.pallas_call(functools.partial(kernel, n_ax, n_xs, chunk), out_shape=ja...]
where the time goes in v2:
time: 45.3 us; the launch traced here: 45.1 us
  Pallas kernels  42.5 us (94%)
  local copies, waits for them, and re-layouts  2.65 us (6%)
    pallas_call x1, Pallas kernels, on_device(): pl.pallas_call(functools.partial(kernel, n_ax, n_xs, chunk), out_shape=ja...  42.5 us
    unnamed x1, local copies, waits for them, and re-layouts  2.65 us

profile of v2, /device:TPU:0, one launch (start us, length us, event | category | flops | bytes accessed | tf_op | source)
XLA Modules:
  0.0 45.1 jit_solution(6728835012133681830)
XLA Ops:
  0.0 42.5 %shard_map.73 = f32[32,32,384]{2,1,0:T(8,128)} custom-call(f32[32,32,384]{2,1,0:T(8,128)} %conc_hbm.1, s32[32,32,384]{2,1,0:T(8,128)} %mask_hbm.1, s32[32,32,384]{2,1,0:T(8,128)} %layer_hbm.1, f32[32,32,384]{2,1,0:T(8,128)} %stiff_hbm.1, f32[32,32,384]{2,1,0:T(8,128)} %prod_hbm.1, f32[4]{0:T(128)} %diff_tab.1, f32[4]{0:T(128)} %upt_tab.1), custom_call_target="tpu_custom_call" | custom-call | tf_op jit(solution)/shard_map/pallas_call | solution.py:395
  42.5 2.7 %copy.9 = f32[32,32,384]{2,1,0:T(8,128)} copy(f32[32,32,384]{2,1,0:T(8,128)} %shard_map.73) | data formatting | bytes 3145728

commit v3 on v2

--- a/solution.py
+++ b/solution.py
@@ -141,6 +141,17 @@
 
     lax.fori_loop(1, m - 1, root_body, 0, unroll=6)
     xs_start(STEPS)
+    col_at = lax.broadcasted_iota(jnp.int32, (slab, cols), 1)
+
+    def plane_body(z, carry):
+        value = root[z + 1]
+        scaled = SECTION_RATE * value
+        plane[z] = scaled * pltpu.roll(value, 1, 0)
+        side[z] = jnp.where(col_at == 0, 0.0, scaled * pltpu.roll(value, 1, 1))
+        return carry
+
+    lax.fori_loop(0, m, plane_body, 0, unroll=8)
+
     for at in range(2):
         @pl.when(sides[2 + at][0])
         def _(at=at):
@@ -172,20 +183,11 @@
     fixed[2] = jnp.where(lower, beta_low, alpha_high)
     fixed[3] = jnp.where(lower, beta_high, alpha_low)
 
-    xs_wait(STEPS)
-    row_at = lax.broadcasted_iota(jnp.int32, (slab, cols), 0)
-    col_at = lax.broadcasted_iota(jnp.int32, (slab, cols), 1)
-
-    def plane_body(z, carry):
-        value = root[z + 1]
-        scaled = SECTION_RATE * value
-        above = jnp.where(row_at == 0, halo[STEPS, 0, z], pltpu.roll(value, 1, 0))
-        plane[z] = scaled * above
+    def fix_body(z, carry):
+        scaled = SECTION_RATE * root[z + 1]
+        plane[z, 0:1] = scaled[0:1] * halo[STEPS, 0, z]
         shut[z] = scaled[slab - 1:slab] * halo[STEPS, 1, z]
-        side[z] = jnp.where(col_at == 0, 0.0, scaled * pltpu.roll(value, 1, 1))
         return carry
-
-    lax.fori_loop(0, m, plane_body, 0, unroll=8)
 
     def a_copy(step, c, to_middle):
         cut = pl.ds(c * chunk, chunk)
@@ -291,6 +293,9 @@
                 for c in early:
                     inward(c)
 
+        if step == 0:
+            xs_wait(STEPS)
+            lax.fori_loop(0, m, fix_body, 0, unroll=8)
         xs_wait(step)
         forward(ends)
         if step == 0:

time: 45.3 us -> 43.8 us (0.967)
  Pallas kernels: 42.5 us -> 41 us
    pallas_call x1, Pallas kernels: 42.5 us -> 41 us  [on_device(): pl.pallas_call(functools.partial(kernel, n_ax, n_xs, chunk), out_shape=ja...]
where the time goes in v3:
time: 43.8 us; the launch traced here: 43.7 us
  Pallas kernels  41 us (94%)
  local copies, waits for them, and re-layouts  2.65 us (6%)
    pallas_call x1, Pallas kernels, on_device(): pl.pallas_call(functools.partial(kernel, n_ax, n_xs, chunk), out_shape=ja...  41 us
    unnamed x1, local copies, waits for them, and re-layouts  2.65 us

profile of v3, /device:TPU:0, one launch (start us, length us, event | category | flops | bytes accessed | tf_op | source)
XLA Modules:
  0.0 43.7 jit_solution(17925934168815225258)
XLA Ops:
  0.0 41.0 %shard_map.73 = f32[32,32,384]{2,1,0:T(8,128)} custom-call(f32[32,32,384]{2,1,0:T(8,128)} %conc_hbm.1, s32[32,32,384]{2,1,0:T(8,128)} %mask_hbm.1, s32[32,32,384]{2,1,0:T(8,128)} %layer_hbm.1, f32[32,32,384]{2,1,0:T(8,128)} %stiff_hbm.1, f32[32,32,384]{2,1,0:T(8,128)} %prod_hbm.1, f32[4]{0:T(128)} %diff_tab.1, f32[4]{0:T(128)} %upt_tab.1), custom_call_target="tpu_custom_call" | custom-call | tf_op jit(solution)/shard_map/pallas_call | solution.py:400
  41.0 2.7 %copy.9 = f32[32,32,384]{2,1,0:T(8,128)} copy(f32[32,32,384]{2,1,0:T(8,128)} %shard_map.73) | data formatting | bytes 3145728

commit v4 on v3

--- a/solution.py
+++ b/solution.py
@@ -132,7 +132,7 @@
         edge[0, 1, z] = state[z, slab - 1:slab]
         return carry
 
-    lax.fori_loop(0, m, copy_edges, 0, unroll=8)
+    lax.fori_loop(0, m, copy_edges, 0, unroll=16)
     xs_start(0)
 
     def root_body(z, carry):
@@ -150,7 +150,7 @@
         side[z] = jnp.where(col_at == 0, 0.0, scaled * pltpu.roll(value, 1, 1))
         return carry
 
-    lax.fori_loop(0, m, plane_body, 0, unroll=8)
+    lax.fori_loop(0, m, plane_body, 0, unroll=16)
 
     for at in range(2):
         @pl.when(sides[2 + at][0])
@@ -173,7 +173,7 @@
         return 1.0 + ratio_now * excess, product * ratio_now, total + product * scaled
 
     ones = jnp.ones((slab, cols), jnp.float32)
-    _, through_up, total = lax.fori_loop(0, m, factor_body, (1.0 + band_first, ones, 0.0 * ones), unroll=8)
+    _, through_up, total = lax.fori_loop(0, m, factor_body, (1.0 + band_first, ones, 0.0 * ones), unroll=16)
     alpha_low = band_first * total
     alpha_high = through_up
     beta_low = band_first * prodr[m - 1]
@@ -217,7 +217,7 @@
         return carry
 
     def cell_loop():
-        lax.fori_loop(0, m, cell_body, 0, unroll=8)
+        lax.fori_loop(0, m, cell_body, 0, unroll=16)
 
     if chunks > 2:
         inside = ((chunk, slab - chunk),)
@@ -253,7 +253,7 @@
                 return tuple(done)
 
             zeros = [jnp.zeros((hi - lo, cols), jnp.float32) for lo, hi in ranges]
-            sums = lax.fori_loop(0, m, body, tuple((zero, zero) for zero in zeros), unroll=8)
+            sums = lax.fori_loop(0, m, body, tuple((zero, zero) for zero in zeros), unroll=16)
             for (lo, hi), (_, first) in zip(ranges, sums):
                 span = slice(lo, hi)
                 last = part[m - 1, span]
@@ -295,7 +295,7 @@
 
         if step == 0:
             xs_wait(STEPS)
-            lax.fori_loop(0, m, fix_body, 0, unroll=8)
+            lax.fori_loop(0, m, fix_body, 0, unroll=16)
         xs_wait(step)
         forward(ends)
         if step == 0:
@@ -367,7 +367,7 @@
                     done.append(solved)
                 return tuple(done)
 
-            lax.fori_loop(0, m, body, tuple(highs), unroll=8)
+            lax.fori_loop(0, m, body, tuple(highs), unroll=16)
 
         if final:
             backward(((0, slab),))

time: 43.8 us -> 45.2 us (1.032)
  Pallas kernels: 41 us -> 42.4 us
    pallas_call x1, Pallas kernels: 41 us -> 42.4 us  [on_device(): pl.pallas_call(functools.partial(kernel, n_ax, n_xs, chunk), out_shape=ja...]
where the time goes in v4:
time: 45.2 us; the launch traced here: 45.1 us
  Pallas kernels  42.4 us (94%)
  local copies, waits for them, and re-layouts  2.65 us (6%)
    pallas_call x1, Pallas kernels, on_device(): pl.pallas_call(functools.partial(kernel, n_ax, n_xs, chunk), out_shape=ja...  42.4 us
    unnamed x1, local copies, waits for them, and re-layouts  2.65 us

profile of v4, /device:TPU:0, one launch (start us, length us, event | category | flops | bytes accessed | tf_op | source)
XLA Modules:
  0.0 45.1 jit_solution(16881695113029967338)
XLA Ops:
  0.0 42.4 %shard_map.73 = f32[32,32,384]{2,1,0:T(8,128)} custom-call(f32[32,32,384]{2,1,0:T(8,128)} %conc_hbm.1, s32[32,32,384]{2,1,0:T(8,128)} %mask_hbm.1, s32[32,32,384]{2,1,0:T(8,128)} %layer_hbm.1, f32[32,32,384]{2,1,0:T(8,128)} %stiff_hbm.1, f32[32,32,384]{2,1,0:T(8,128)} %prod_hbm.1, f32[4]{0:T(128)} %diff_tab.1, f32[4]{0:T(128)} %upt_tab.1), custom_call_target="tpu_custom_call" | custom-call | tf_op jit(solution)/shard_map/pallas_call | solution.py:400
  42.4 2.7 %copy.9 = f32[32,32,384]{2,1,0:T(8,128)} copy(f32[32,32,384]{2,1,0:T(8,128)} %shard_map.73) | data formatting | bytes 3145728
